TPU v7x, 256 devices: a whole 4x4x8 slice. The times are simulated.
256 devices in a mesh: node: 4 (over z_lo), space: 64 (over y, z_hi, x, core).
Axes of the slice: x: 4, y: 4, z: 8 (z_hi: 2, z_lo: 4; z = z_hi * 4 + z_lo), core: 2. Of those that a mesh axis runs over, the one named last changes fastest.
Arguments:
- start_state: float32 [5, 4, 4, 4, 64, 1280], P(None, None, None, None, 'space'), may hold values from -1.5 to 14, as said below
- node_offset: float32 [4, 5, 4, 4, 4, 64, 1280], P('node', None, None, None, None, 'space'), may hold values from -0.6 to 0.6
Outputs:
- increments: float32 [4, 5, 4, 4, 4, 64, 1280], P('node', None, None, None, None, 'space')
Inputs may be any that keep to these rules, and one draw needn't show every extreme that they name: `start_state`: conserved variables of a gas with gamma 1.4, density and pressure between 2 and 5 and every velocity component within 0.3 in magnitude, drawn independently at each node.
All inputs are finite; a program needn't handle non-finite values.
Results may differ from a plain program's by a relative error of at most 0.0001.
Values sent between devices are 32-bit elements; how exact they have to be, the bound alone decides.
A program may use at most 64 MiB of HBM per device.

v0:
```python
import math

import jax
import jax.numpy as jnp
import numpy as np
from jax import lax
from jax.sharding import PartitionSpec as P

EZ = 80
ITERS = 2


gamma_gas = 1.4
step_length = 0.01
inverse_weight = 6.0
highest = lax.Precision.HIGHEST
derivative_forms = ("ia,vabcxp->vibcxp", "ib,vabcxp->vaicxp", "ic,vabcxp->vabixp")


def shifted(block, axis, distance):
    devices = range(lax.axis_size(axis))
    route = [((i - distance) % len(devices), i) for i in devices]
    return lax.ppermute(block, axis, route)


def lobatto_derivative():
    points = np.array([-1.0, -math.sqrt(0.2), math.sqrt(0.2), 1.0])
    barycentric = np.ones(4)
    for i in range(4):
        for k in range(4):
            if k != i:
                barycentric[i] = barycentric[i] / (points[i] - points[k])
    derivative = np.zeros((4, 4))
    for i in range(4):
        for j in range(4):
            if i != j:
                derivative[i, j] = barycentric[j] / barycentric[i] / (points[i] - points[j])
        derivative[i, i] = -np.sum(derivative[i])
    return derivative


def collocation_matrix():
    near_root = math.sqrt(3.0 / 7 - 2.0 / 7 * math.sqrt(1.2))
    far_root = math.sqrt(3.0 / 7 + 2.0 / 7 * math.sqrt(1.2))
    time_nodes = [(1.0 + value) / 2 for value in (-far_root, -near_root, near_root, far_root)]
    quad_table = np.zeros((4, 4))
    for j in range(4):
        coeffs = [1.0]
        for k in range(4):
            if k != j:
                scale = 1.0 / (time_nodes[j] - time_nodes[k])
                widened = [0.0] * (len(coeffs) + 1)
                for power in range(len(coeffs)):
                    widened[power + 1] = widened[power + 1] + coeffs[power] * scale
                    widened[power] = widened[power] - time_nodes[k] * coeffs[power] * scale
                coeffs = widened
        for m in range(4):
            total = 0.0
            for power in range(len(coeffs)):
                total = total + coeffs[power] * time_nodes[m] ** (power + 1) / (power + 1)
            quad_table[m, j] = total
    return quad_table


def physical_flux(state, direction):
    density = state[0]
    momenta = state[1:4]
    energy = state[4]
    velocity = momenta / density
    pressure = (gamma_gas - 1.0) * (energy - 0.5 * jnp.sum(momenta * velocity, axis=0))
    normal_speed = velocity[direction]
    columns = [momenta[direction]]
    for component in range(3):
        entry = momenta[component] * normal_speed
        if component == direction:
            entry = entry + pressure
        columns.append(entry)
    columns.append((energy + pressure) * normal_speed)
    return (jnp.stack(columns), jnp.abs(normal_speed) + jnp.sqrt(gamma_gas * pressure / density))


def face_flux(left_state, right_state, direction):
    left_flux, left_wave = physical_flux(left_state, direction)
    right_flux, right_wave = physical_flux(right_state, direction)
    wave_speed = jnp.maximum(left_wave, right_wave)
    return 0.5 * (left_flux + right_flux) - 0.5 * wave_speed * (right_state - left_state)


def edge_slice(array, dim, first):
    return lax.slice_in_dim(array, first, first + 1, axis=dim)


def with_surface(first_term, last_term, dim):
    filler = jnp.zeros_like(first_term)
    return jnp.concatenate([first_term, filler, filler, last_term], axis=dim)


def next_element(array, direction, column):
    if direction == 1:
        return jnp.roll(array, -EZ, axis=5)
    return jnp.where(column == EZ - 1, jnp.roll(array, EZ - 1, axis=5), jnp.roll(array, -1, axis=5))


def prior_element(array, direction, column):
    if direction == 1:
        return jnp.roll(array, EZ, axis=5)
    return jnp.where(column == 0, jnp.roll(array, 1 - EZ, axis=5), jnp.roll(array, 1, axis=5))


def element_rate(state):
    slab_width = state.shape[4]
    plane_size = state.shape[5]
    column = jnp.arange(plane_size, dtype=jnp.int32) % EZ
    derivative = jnp.asarray(lobatto_derivative(), jnp.float32)
    total_rate = jnp.zeros_like(state)
    for direction in range(3):
        flux, wave_unused = physical_flux(state, direction)
        total_rate = total_rate - jnp.einsum(
            derivative_forms[direction], derivative, flux, precision=highest
        )
        node_dim = 1 + direction
        own_first = edge_slice(state, node_dim, 0)
        own_last = edge_slice(state, node_dim, 3)
        if direction == 0:
            trace_shape = own_last.shape[:4] + (1, plane_size)
            flat_shape = (own_last.shape[0], 16, plane_size)
            last_edge = own_last.reshape(flat_shape)
            first_edge = own_first.reshape(flat_shape)
            from_left = shifted(last_edge, "space", 1).reshape(trace_shape)
            from_right = shifted(first_edge, "space", -1).reshape(trace_shape)
            left_states = jnp.concatenate([from_left, own_last], axis=4)
            right_states = jnp.concatenate([own_first, from_right], axis=4)
            all_faces = face_flux(left_states, right_states, 0)
            left_faces = lax.slice_in_dim(all_faces, 0, slab_width, axis=4)
            right_faces = lax.slice_in_dim(all_faces, 1, slab_width + 1, axis=4)
        else:
            right_faces = face_flux(own_last, next_element(own_first, direction, column), direction)
            left_faces = prior_element(right_faces, direction, column)
        flux_first = edge_slice(flux, node_dim, 0)
        flux_last = edge_slice(flux, node_dim, 3)
        total_rate = total_rate + inverse_weight * with_surface(
            left_faces - flux_first, flux_last - right_faces, node_dim
        )
    return total_rate


def node_quadrature(node_rate, quad_table, node_rank):
    weights = quad_table[node_rank]
    return jnp.tensordot(
        weights,
        lax.all_gather(node_rate[None], "node", axis=0, tiled=True),
        axes=1,
        precision=highest,
    )


def body(start_state, node_offset):
    quad_table = jnp.asarray(collocation_matrix(), jnp.float32)
    node_rank = lax.axis_index("node")
    node_state = start_state + node_offset[0]
    increment = jnp.zeros_like(start_state)
    for iteration in range(ITERS):
        node_rate = element_rate(node_state)
        increment = step_length * node_quadrature(node_rate, quad_table, node_rank)
        node_state = start_state + increment
    return increment[None]


def solution(mesh):
    return jax.shard_map(
        body,
        mesh=mesh,
        in_specs=(
            P(None, None, None, None, "space", None),
            P("node", None, None, None, None, "space", None),
        ),
        out_specs=P("node", None, None, None, None, "space", None),
        check_vma=False,
    )
```

profile of v0, /device:TPU:32, one launch (start us, length us, event | category | flops | bytes accessed | tf_op | source)
XLA Modules:
  0.0 420.0 jit_solution(15142015382553567652)
XLA Ops:
  6.5 2.6 bitcast_add_fusion
  10.3 10.8 %collective-permute-start.1 = (f32[5,16,1280]{2,1,0:T(8,128)}, f32[5,16,1280]{2,1,0:T(8,128)}, u32[]{:S(2)}, u32[]{:S(2)}) collective-permute-start(f32[5,16,1280]{2,1,0:T(8,128)} %reshape.2282), channel_id=1, source_target_pairs={{1,0},{2,1},{3,2},{4,3},{5,4},{6,5},{7,6},{8,7},{9,8},{10,9},{11,1... | collective-permute-start | bytes 1228808 | tf_op jit(solution)/shard_map/ppermute | solution.py:23
  29.1 1.2 copy-done.7
  30.2 1.5 slice_subtract_fusion.6
  35.3 1.3 fusion.40
  36.6 4.0 fusion.19
  44.1 4.4 %fusion.24 = f32[5,4,4,1280,4]{3,4,2,1,0:T(4,128)} fusion(f32[4,4,1,1,1]{1,0,4,3,2:T(4,128)S(1)} %copy-done.18, f32[5,4,4,4,1280]{4,3,1,2,0:T(4,128)S(1)} %bitcast.577), kind=kOutput, calls=%fused_computation.36 | convolution fusion | flops 19660800 | bytes 3276864 | tf_op jit(solution)/shard_map/ib,vabcxp->vaicxp/dot_general | solution.py:118
  48.9 1.1 reshape.2283
  55.1 5.6 %fusion.15 = f32[5,4,4,4,1,1280]{5,1,3,2,0,4:T(4,128)S(1)} fusion(f32[4,4,1,1,1]{1,0,4,3,2:T(4,128)S(1)} %copy-done.18, f32[5,1,4,4,1,1280]{5,1,3,2,0,4:T(1,128)S(1)} %copy.313, f32[5,1,4,4,1,1280]{5,1,3,2,0,4:T(1,128)S(1)} %copy.312, f32[5,4,1,4,1,1280]{5,1,3,2,0,4:T(4,128)S(1)} %copy-done.17, f32[5,4,1,4,1,1280]{5,1,3,2,0,4:T(4,128)S(1)} %copy-done.16, ...), kind=kOutput, calls=%fused_computation.17 | convolution fusion | flops 25804800 | bytes 9011280 | tf_op jit(solution)/shard_map/ia,vabcxp->vibcxp/dot_general | solution.py:118
  60.7 1.6 copy.368
  62.6 120.3 %all-gather.5.cloned.1.call-done = f32[20,4,4,4,1,1280]{5,3,4,2,1,0:T(4,128)} async-done(((f32[5,4,4,4,1,1280]{5,3,4,2,1,0:T(4,128)}), f32[20,4,4,4,1,1280]{5,3,4,2,1,0:T(4,128)}) %all-gather.5.cloned.1.call-update) | async-done | bytes 6553616 | tf_op jit(solution)/shard_map/all_gather | solution.py:151
  182.9 19.7 %fusion.2 = f32[1,5,4,4,4,1280]{5,0,4,3,2,1:T(1,128)S(1)} fusion(f32[4,5,4,4,4,1280]{5,4,3,2,1,0:T(4,128)} %bitcast.574, f32[4,4]{1,0:T(4,128)S(1)} %copy-done.19, s32[]{:T(128)S(6)} %select_n.64), kind=kOutput, calls=%fused_computation.2 | convolution fusion | flops 19660800 | bytes 8192516 | tf_op jit(solution)/shard_map/dot_general | solution.py:149
  210.6 1.3 multiply_add_fusion
  212.1 1.5 slice_subtract_fusion
  214.7 4.2 fusion.17
  225.9 4.4 %fusion.21 = f32[5,4,4,1280,4]{3,4,2,1,0:T(4,128)} fusion(f32[4,4,1,1,1]{1,0,4,3,2:T(4,128)S(1)} %copy-done.18, f32[5,4,4,4,1280]{4,3,1,2,0:T(4,128)S(1)} %bitcast.576), kind=kOutput, calls=%fused_computation.33 | convolution fusion | flops 19660800 | bytes 3276864 | tf_op jit(solution)/shard_map/ib,vabcxp->vaicxp/dot_general | solution.py:118
  232.2 10.0 %collective-permute-start.3 = (f32[5,16,1280]{2,1,0:T(8,128)}, f32[5,16,1280]{2,1,0:T(8,128)}, u32[]{:S(2)}, u32[]{:S(2)}) collective-permute-start(f32[5,16,1280]{2,1,0:T(8,128)} %reshape.2290), channel_id=1, source_target_pairs={{1,0},{2,1},{3,2},{4,3},{5,4},{6,5},{7,6},{8,7},{9,8},{10,9},{11,1... | collective-permute-start | bytes 1228808 | tf_op jit(solution)/shard_map/ppermute | solution.py:23
  242.2 1.7 copy_dynamic-update-slice_fusion.5
  246.3 5.3 %collective-permute-done.2 = f32[5,16,1280]{2,1,0:T(8,128)} collective-permute-done((f32[5,16,1280]{2,1,0:T(8,128)}, f32[5,16,1280]{2,1,0:T(8,128)}, u32[]{:S(2)}, u32[]{:S(2)}) %collective-permute-start.2) | collective-permute-done | bytes 409632 | tf_op jit(solution)/shard_map/ppermute | solution.py:23
  259.3 6.1 %fusion.10 = f32[5,4,4,4,1,1280]{5,1,3,2,0,4:T(4,128)S(1)} fusion(f32[4,4,1,1,1]{1,0,4,3,2:T(4,128)S(1)} %copy-done.18, f32[5,1,4,4,1,1280]{5,1,3,2,0,4:T(1,128)S(1)} %copy.404, f32[5,1,4,4,1,1280]{5,1,3,2,0,4:T(1,128)S(1)} %copy.403, f32[5,4,1,4,1,1280]{5,1,3,2,0,4:T(4,128)S(1)} %copy-done.13, f32[5,4,1,4,1,1280]{5,1,3,2,0,4:T(4,128)S(1)} %copy-done.12, ...), kind=kOutput, calls=%fused_computation.12 | convolution fusion | flops 25804800 | bytes 9011280 | tf_op jit(solution)/shard_map/ia,vabcxp->vibcxp/dot_general | solution.py:118
  265.3 1.6 copy.447
  267.0 123.1 %all-gather.7.cloned.1.call-done = f32[20,4,4,4,1,1280]{5,3,4,2,1,0:T(4,128)} async-done(((f32[5,4,4,4,1,1280]{5,3,4,2,1,0:T(4,128)}), f32[20,4,4,4,1,1280]{5,3,4,2,1,0:T(4,128)}) %all-gather.7.cloned.1.call-update) | async-done | bytes 6553616 | tf_op jit(solution)/shard_map/all_gather | solution.py:151
  390.1 19.4 %fusion = f32[1,5,4,4,4,1280]{5,0,4,3,2,1:T(1,128)S(1)} fusion(f32[4,5,4,4,4,1280]{5,4,3,2,1,0:T(4,128)} %bitcast.575, f32[4,4]{1,0:T(4,128)S(1)} %copy-done.19, s32[]{:T(128)S(6)} %select_n.64), kind=kOutput, calls=%fused_computation | convolution fusion | flops 19660800 | bytes 8192516 | tf_op jit(solution)/shard_map/dot_general | solution.py:149
  410.0 2.8 copy.448
  (226 shorter events, 49.9 us)
Async XLA Ops:
  6.5 176.4 %all-gather.5.cloned.1.call-start = ((), (), s32[]{:S(2)}) async-start(), calls=%async_computation | async-start | bytes 8192000 | tf_op jit(solution)/shard_map/all_gather | solution.py:151
  9.3 39.2 %collective-permute-start = (f32[5,16,1280]{2,1,0:T(8,128)S(1)}, f32[5,16,1280]{2,1,0:T(8,128)S(1)}, u32[]{:S(2)}, u32[]{:S(2)}) collective-permute-start(f32[5,16,1280]{2,1,0:T(8,128)S(1)} %reshape.2280), channel_id=1, source_target_pairs={{63,0},{0,1},{1,2},{2,3},{3,4},{4,5},{5,6},{6,7},{7,8},{8,9},{9,10... | collective-permute-start | bytes 1228808 | tf_op jit(solution)/shard_map/ppermute | solution.py:23
  10.3 38.6 %collective-permute-start.1 = (f32[5,16,1280]{2,1,0:T(8,128)}, f32[5,16,1280]{2,1,0:T(8,128)}, u32[]{:S(2)}, u32[]{:S(2)}) collective-permute-start(f32[5,16,1280]{2,1,0:T(8,128)} %reshape.2282), channel_id=1, source_target_pairs={{1,0},{2,1},{3,2},{4,3},{5,4},{6,5},{7,6},{8,7},{9,8},{10,9},{11,1... | collective-permute-start | bytes 1228808 | tf_op jit(solution)/shard_map/ppermute | solution.py:23
  25.3 1.4 copy-start.2
  34.9 1.7 copy-start.18
  51.5 1.4 copy-start.8
  51.5 2.6 copy-start.16
  51.5 2.6 copy-start.17
  52.9 1.5 copy-start.5
  52.9 2.0 copy-start.6
  52.9 2.0 copy-start.14
  52.9 2.1 copy-start.15
  62.3 120.6 %copy-start.19 = (f32[4,4]{1,0:T(4,128)S(1)}, f32[4,4]{1,0:T(4,128)}, u32[]{:S(2)}) copy-start(f32[4,4]{1,0:T(4,128)} %constant.70.clone) | copy-start | bytes 196
  62.3 327.7 %all-gather.7.cloned.1.call-start = ((), (), s32[]{:S(2)}) async-start(), calls=%async_computation.1 | async-start | bytes 8192000 | tf_op jit(solution)/shard_map/all_gather | solution.py:151
  182.9 19.7 %copy-start = (f32[5,4,4,4,1,1280]{5,4,3,2,1,0:T(1,128)S(1)}, f32[5,4,4,4,1,1280]{5,4,3,2,1,0:T(1,128)}, u32[]{:S(2)}) copy-start(f32[5,4,4,4,1,1280]{5,4,3,2,1,0:T(1,128)} %param.5) | copy-start | bytes 4915204
  231.2 20.4 %collective-permute-start.2 = (f32[5,16,1280]{2,1,0:T(8,128)}, f32[5,16,1280]{2,1,0:T(8,128)}, u32[]{:S(2)}, u32[]{:S(2)}) collective-permute-start(f32[5,16,1280]{2,1,0:T(8,128)} %reshape.2288), channel_id=1, source_target_pairs={{63,0},{0,1},{1,2},{2,3},{3,4},{4,5},{5,6},{6,7},{7,8},{8,9},{9,10... | collective-permute-start | bytes 1228808 | tf_op jit(solution)/shard_map/ppermute | solution.py:23
  232.2 20.8 %collective-permute-start.3 = (f32[5,16,1280]{2,1,0:T(8,128)}, f32[5,16,1280]{2,1,0:T(8,128)}, u32[]{:S(2)}, u32[]{:S(2)}) collective-permute-start(f32[5,16,1280]{2,1,0:T(8,128)} %reshape.2290), channel_id=1, source_target_pairs={{1,0},{2,1},{3,2},{4,3},{5,4},{6,5},{7,6},{8,7},{9,8},{10,9},{11,1... | collective-permute-start | bytes 1228808 | tf_op jit(solution)/shard_map/ppermute | solution.py:23
  255.7 1.4 copy-start.9
  255.7 2.6 copy-start.12
  255.7 2.6 copy-start.13
  257.1 1.5 copy-start.3
  257.1 2.0 copy-start.4
  257.1 2.0 copy-start.10
  257.1 2.1 copy-start.11
  (3 other events, 2.9 us)
Sparse Core Ops, SparseCore 0:
  62.5 120.3 all-gather.4
  267.1 122.9 all-gather.6
where the time goes:
time: 424 us; the launch traced here: 420 us
  waiting for transfers between devices  249 us (59%)
  matrix products  67.7 us (16%)
  local copies, waits for them, and re-layouts  38.9 us (9%)
  other arithmetic  28.8 us (7%)
  starting transfers between devices  21.2 us (5%)
  between operations  14.6 us (3%)
    all_gather x2, waiting for transfers between devices, node_quadrature(): lax.all_gather(node_rate[None], 'node', axis=0, tiled=True)  243 us
    dot_general x2, matrix products, node_quadrature(): jnp.tensordot(weights, lax.all_gather(node_rate[None], 'node', axis=0, ti...  39.1 us
    dot_general x6, matrix products, element_rate(): jnp.einsum(derivative_forms[direction], derivative, flux, precision=highest)  28.6 us
    ppermute x4, starting transfers between devices, shifted(): return lax.ppermute(block, axis, route)  21 us
    unnamed x72, local copies, waits for them, and re-layouts  10.3 us
  transfers between devices with their start and end apart: 6, of which 3 were waited for; matrix products, arithmetic and copies ran while one was open for 8% of the time, Pallas kernels for 0%

commit v1 on v0

v1 whole, which is shorter than its diff:
```python
import functools
import math

import jax
import jax.numpy as jnp
import numpy as np
from jax import lax
from jax.experimental import pallas as pl
from jax.experimental.pallas import tpu as pltpu
from jax.sharding import PartitionSpec as P

MESH = pl.DeviceIdType.MESH
TILES = 10
GAS = 1.4
STEP = 0.01


def lobatto_derivative():
    points = np.array([-1.0, -math.sqrt(0.2), math.sqrt(0.2), 1.0])
    barycentric = np.ones(4)
    for i in range(4):
        for k in range(4):
            if k != i:
                barycentric[i] = barycentric[i] / (points[i] - points[k])
    derivative = np.zeros((4, 4))
    for i in range(4):
        for j in range(4):
            if i != j:
                derivative[i, j] = barycentric[j] / barycentric[i] / (points[i] - points[j])
        derivative[i, i] = -np.sum(derivative[i])
    return derivative


def collocation_matrix():
    near_root = math.sqrt(3.0 / 7 - 2.0 / 7 * math.sqrt(1.2))
    far_root = math.sqrt(3.0 / 7 + 2.0 / 7 * math.sqrt(1.2))
    time_nodes = [(1.0 + value) / 2 for value in (-far_root, -near_root, near_root, far_root)]
    quad_table = np.zeros((4, 4))
    for j in range(4):
        coeffs = [1.0]
        for k in range(4):
            if k != j:
                scale = 1.0 / (time_nodes[j] - time_nodes[k])
                widened = [0.0] * (len(coeffs) + 1)
                for power in range(len(coeffs)):
                    widened[power + 1] = widened[power + 1] + coeffs[power] * scale
                    widened[power] = widened[power] - time_nodes[k] * coeffs[power] * scale
                coeffs = widened
        for m in range(4):
            total = 0.0
            for power in range(len(coeffs)):
                total = total + coeffs[power] * time_nodes[m] ** (power + 1) / (power + 1)
            quad_table[m, j] = total
    return quad_table


D = [[float(value) for value in row] for row in lobatto_derivative()]
Q = [[float(STEP * value) for value in row] for row in collocation_matrix()]


def lanes():
    return lax.broadcasted_iota(jnp.int32, (8, 128), 1)


def upper_half():
    return lax.broadcasted_iota(jnp.int32, (8, 128), 0) < 4


def swap(value):
    return pltpu.roll(value, 4, 0)


def turn(value, shift):
    return pltpu.roll(value, shift, 1)


def primitives(state, direction):
    inverse = 1.0 / state[0]
    speeds = [state[1 + k] * inverse for k in range(3)]
    kinetic = state[1] * speeds[0] + state[2] * speeds[1] + state[3] * speeds[2]
    pressure = (GAS - 1.0) * (state[4] - 0.5 * kinetic)
    return inverse, speeds[direction], pressure


def fluxes(state, speed, pressure, direction):
    columns = [state[1 + direction]]
    for k in range(3):
        entry = state[1 + k] * speed
        columns.append(entry + pressure if k == direction else entry)
    columns.append((state[4] + pressure) * speed)
    return columns


def wave(inverse, speed, pressure):
    return jnp.abs(speed) + jnp.sqrt(GAS * pressure * inverse)


def lift(own, own_flux, own_wave, other, direction, sign):
    inverse, speed, pressure = primitives(other, direction)
    other_flux = fluxes(other, speed, pressure, direction)
    top = jnp.maximum(own_wave, wave(inverse, speed, pressure))
    return [
        3.0 * (sign * (other_flux[v] - own_flux[v]) + top * (other[v] - own[v])) for v in range(5)
    ]


def derivative(values):
    out = []
    for i in range(4):
        row = []
        for v in range(5):
            total = None
            for j in range(4):
                if abs(D[i][j]) > 1e-12:
                    term = (-D[i][j]) * values[j][v]
                    total = term if total is None else total + term
            row.append(total)
        out.append(row)
    return out


def strided(ref, at, v, pair, c):
    return ref[at, v, pl.ds(32 * pair + c, 8, 4), :]


def rows(ref, at, v, start):
    return ref[at, v, pl.ds(start, 8), :]


def pass_z(u, at, before, after, out, to, tile):
    lane = lanes()
    base = lax.rem(48 * tile, 80)
    place = lane + base
    first = (place == 0) | (place == 80) | (place == 160)
    last = (place == 79) | (place == 159)
    for pair in range(2):
        state = [[strided(u, at, v, pair, c) for v in range(5)] for c in range(4)]
        prims = [primitives(state[c], 2) for c in range(4)]
        flux = [fluxes(state[c], prims[c][1], prims[c][2], 2) for c in range(4)]
        rate = derivative(flux)
        left = []
        right = []
        for v in range(5):
            back = strided(u, before, v, pair, 3)
            ahead = strided(u, after, v, pair, 3)
            near = turn(jnp.where(lane == 127, back, state[3][v]), 1)
            far = turn(jnp.where(lane >= 79, state[3][v], ahead), 49)
            left.append(jnp.where(first, far, near))
            back = strided(u, before, v, pair, 0)
            ahead = strided(u, after, v, pair, 0)
            near = turn(jnp.where(lane == 0, ahead, state[0][v]), 127)
            far = turn(jnp.where(lane >= 49, back, state[0][v]), 79)
            right.append(jnp.where(last, far, near))
        low = lift(state[0], flux[0], wave(*prims[0]), left, 2, 1.0)
        high = lift(state[3], flux[3], wave(*prims[3]), right, 2, -1.0)
        for v in range(5):
            for c in range(4):
                value = rate[c][v]
                if c == 0:
                    value = value + low[v]
                if c == 3:
                    value = value + high[v]
                out[to, v, pl.ds(32 * pair + c, 8, 4), :] = value


def pass_y(u, at, before, after, out, to):
    lane = lanes()
    half = upper_half()
    sign = jnp.where(half, 1.0, -1.0).astype(jnp.float32)

    def two(x, y):
        return jnp.where(half, jnp.float32(-x), jnp.float32(-y))

    mix_low = [two(D[0][0], D[1][1]), two(D[0][1], D[1][0]), two(D[0][2], D[1][3]), two(D[0][3], D[1][2])]
    mix_high = [two(D[2][0], D[3][1]), two(D[2][1], D[3][0]), two(D[2][2], D[3][3]), two(D[2][3], D[3][2])]
    for a in range(4):
        low = [rows(u, at, v, 16 * a) for v in range(5)]
        high = [rows(u, at, v, 16 * a + 8) for v in range(5)]
        prim_low = primitives(low, 1)
        prim_high = primitives(high, 1)
        flux_low = fluxes(low, prim_low[1], prim_low[2], 1)
        flux_high = fluxes(high, prim_high[1], prim_high[2], 1)
        own = [jnp.where(half, low[v], high[v]) for v in range(5)]
        own_flux = [jnp.where(half, flux_low[v], flux_high[v]) for v in range(5)]
        own_wave = wave(*[jnp.where(half, x, y) for x, y in zip(prim_low, prim_high)])
        other = []
        for v in range(5):
            back = rows(u, before, v, 16 * a + 8)
            ahead = rows(u, after, v, 16 * a)
            down = turn(jnp.where(lane >= 48, back, high[v]), 80)
            up = turn(jnp.where(lane >= 80, low[v], ahead), 48)
            other.append(swap(jnp.where(half, up, down)))
        face = lift(own, own_flux, own_wave, other, 1, sign)
        for v in range(5):
            parts = [flux_low[v], swap(flux_low[v]), flux_high[v], swap(flux_high[v])]
            sum_low = jnp.where(half, face[v], 0.0)
            sum_high = jnp.where(half, 0.0, face[v])
            for k in range(4):
                sum_low = sum_low + mix_low[k] * parts[k]
                sum_high = sum_high + mix_high[k] * parts[k]
            out[to, v, pl.ds(16 * a, 8), :] += sum_low
            out[to, v, pl.ds(16 * a + 8, 8), :] += sum_high


def pass_x(u, at, out, to):
    for h in range(2):
        state = [[rows(u, at, v, 16 * a + 8 * h) for v in range(5)] for a in range(4)]
        flux = []
        for a in range(4):
            _, speed, pressure = primitives(state[a], 0)
            flux.append(fluxes(state[a], speed, pressure, 0))
        rate = derivative(flux)
        for a in range(4):
            for v in range(5):
                out[to, v, pl.ds(16 * a + 8 * h, 8), :] += rate[a][v]


def faces_x(u, at, lower, low_at, upper, up_at, out, to):
    for h in range(2):
        for a, other, sign in ((0, lower, 1.0), (3, upper, -1.0)):
            own = [rows(u, at, v, 16 * a + 8 * h) for v in range(5)]
            inverse, speed, pressure = primitives(own, 0)
            own_flux = fluxes(own, speed, pressure, 0)
            trace = [other(v, h) for v in range(5)]
            face = lift(own, own_flux, wave(inverse, speed, pressure), trace, 0, sign)
            for v in range(5):
                out[to, v, pl.ds(16 * a + 8 * h, 8), :] += face[v]


def inner_rate(u, at, before, after, out, to, tile):
    pass_z(u, at, before, after, out, to, tile)
    pass_y(u, at, before, after, out, to)
    pass_x(u, at, out, to)


def pack(ref, at, side, tile):
    lane = lanes()
    half = upper_half()
    packed = []
    for v in range(5):
        for pair in range(2):
            c0 = strided(ref, at, v, pair, 0)
            c3 = strided(ref, at, v, pair, 3)
            if side == 0:
                one = rows(ref, at, v, 32 * pair + 8)
                two = rows(ref, at, v, 32 * pair + 24)
                main = jnp.where(half, swap(one), two)
                main = jnp.where(lane == 0, turn(c0, 8 + 8 * tile), main)
                main = jnp.where(lane == 1, turn(c3, 2), main)
            else:
                one = rows(ref, at, v, 32 * pair)
                two = rows(ref, at, v, 32 * pair + 16)
                main = jnp.where(half, one, swap(two))
                main = jnp.where(lane == 127, turn(c0, 127), main)
                main = jnp.where(lane == 126, turn(c3, 47 + 8 * tile), main)
            packed.append(main)
    return packed


def unpack(packed, ref, at, side):
    for v in range(5):
        for pair in range(2):
            block = packed[2 * v + pair]
            at0, at3 = (0, 1) if side == 0 else (127, 126)
            c0 = jnp.broadcast_to(block[:, at0 : at0 + 1], (8, 128))
            c3 = jnp.broadcast_to(block[:, at3 : at3 + 1], (8, 128))
            ref[at, v, pl.ds(32 * pair, 8, 4), :] = c0
            ref[at, v, pl.ds(32 * pair + 3, 8, 4), :] = c3
            shift = 12 if side == 0 else 0
            ref[at, v, pl.ds(32 * pair + shift, 4), :] = block[0:4]
            ref[at, v, pl.ds(32 * pair + 16 + shift, 4), :] = block[4:8]


def tile_before(q):
    return 3 * q - 2 + 11 * ((3 - q) // 3)


def tile_after(q):
    return 3 * q + 2 - 11 * (q // 3)


def kernel(
    start_hbm,
    offset_hbm,
    out_hbm,
    start,
    u0,
    x_low,
    x_high,
    rate,
    halo_send,
    landed,
    halo,
    u1,
    x_low2,
    x_high2,
    rate2,
    give,
    load_sem,
    x_send,
    x_recv,
    mid_send,
    mid_recv,
    end_send,
    end_recv,
    halo_ssem,
    halo_rsem,
    own_sem,
    own_halo_sem,
    x_send2,
    x_recv2,
    give_send,
    give_recv,
    give_own,
):
    m = lax.axis_index("node")
    s = lax.axis_index("space")
    hi = (s // 8) % 2
    q = m + hi * (3 - 2 * m)
    up = (s + 1) % 64
    down = (s + 63) % 64
    hi_up = (up // 8) % 2
    hi_down = (down // 8) % 2
    q_up = q + hi_up * (3 - 2 * q)
    q_down = q + hi_down * (3 - 2 * q)
    slot_from = (3 - q) // 3
    slot_to = 3 - q // 3
    first_tile = 3 * q - 1

    def loads(t):
        return (
            pltpu.make_async_copy(start_hbm.at[:, :, t, 0, :], start.at[t], load_sem.at[0, t]),
            pltpu.make_async_copy(offset_hbm.at[:, :, t, 0, :], u0.at[t], load_sem.at[1, t]),
        )

    def begin(t, carry):
        one, two = loads(t)
        one.start()
        two.start()
        return carry

    lax.fori_loop(0, TILES, begin, 0)

    barrier = pltpu.get_barrier_semaphore()
    for k in range(1, 4):
        pl.semaphore_signal(barrier, inc=1, device_id={"node": (m + k) % 4}, device_id_type=MESH)
    pl.semaphore_signal(barrier, inc=1, device_id={"space": up}, device_id_type=MESH)
    pl.semaphore_signal(barrier, inc=1, device_id={"space": down}, device_id_type=MESH)
    pl.semaphore_signal(barrier, inc=1, device_id={"node": q_up, "space": up}, device_id_type=MESH)
    pl.semaphore_signal(barrier, inc=1, device_id={"node": q_down, "space": down}, device_id_type=MESH)
    pl.semaphore_wait(barrier, 7)

    def x_copies(t):
        return (
            pltpu.make_async_remote_copy(
                src_ref=u0.at[t, :, pl.ds(48, 16)],
                dst_ref=x_low.at[t],
                send_sem=x_send.at[0, t],
                recv_sem=x_recv.at[0, t],
                device_id={"space": up},
                device_id_type=MESH,
            ),
            pltpu.make_async_remote_copy(
                src_ref=u0.at[t, :, pl.ds(0, 16)],
                dst_ref=x_high.at[t],
                send_sem=x_send.at[1, t],
                recv_sem=x_recv.at[1, t],
                device_id={"space": down},
                device_id_type=MESH,
            ),
        )

    def guess(t, carry):
        one, two = loads(t)
        one.wait()
        two.wait()
        for v in range(5):
            u0[t, v] = u0[t, v] + start[t, v]
        one, two = x_copies(t)
        one.start()
        two.start()
        return carry

    lax.fori_loop(0, TILES, guess, 0)

    def owner(t):
        d = (t + 1) // 3
        return d, d + hi * (3 - 2 * d)

    def mid_copy(t):
        d, place = owner(t)
        return pltpu.make_async_remote_copy(
            src_ref=rate.at[t, :, pl.ds(16, 32)],
            dst_ref=landed.at[m, t - 3 * d + 1, :, pl.ds(16, 32)],
            send_sem=mid_send.at[t],
            recv_sem=mid_recv.at[m, t - 3 * d + 1],
            device_id={"node": place},
            device_id_type=MESH,
        )

    def end_copies(t):
        d, place = owner(t)
        return [
            pltpu.make_async_remote_copy(
                src_ref=rate.at[t, :, pl.ds(48 * k, 16)],
                dst_ref=landed.at[m, t - 3 * d + 1, :, pl.ds(48 * k, 16)],
                send_sem=end_send.at[k, t],
                recv_sem=end_recv.at[k, m, t - 3 * d + 1],
                device_id={"node": place},
                device_id_type=MESH,
            )
            for k in range(2)
        ]

    def own_copy(slot):
        return pltpu.make_async_copy(
            rate.at[first_tile + slot], landed.at[m, slot], own_sem.at[slot]
        )

    def inside(t, carry):
        inner_rate(u0, t, (t + 9) % 10, (t + 1) % 10, rate, t, t)
        d, place = owner(t)

        @pl.when(d != q)
        def _():
            mid_copy(t).start()

        return carry

    lax.fori_loop(0, TILES, inside, 0)

    def edges(t, carry):
        one, two = x_copies(t)
        one.wait_recv()
        two.wait_recv()
        faces_x(
            u0,
            t,
            lambda v, h: x_low[t, v, pl.ds(8 * h, 8), :],
            t,
            lambda v, h: x_high[t, v, pl.ds(8 * h, 8), :],
            t,
            rate,
            t,
        )
        d, place = owner(t)

        @pl.when(d != q)
        def _():
            for copy in end_copies(t):
                copy.start()

        @pl.when(d == q)
        def _():
            own_copy(t - first_tile).start()

        return carry

    lax.fori_loop(0, TILES, edges, 0)

    def halo_copies(d):
        place = d + hi * (3 - 2 * d)
        return [
            pltpu.make_async_remote_copy(
                src_ref=halo_send.at[d, side],
                dst_ref=halo.at[m, side],
                send_sem=halo_ssem.at[d, side],
                recv_sem=halo_rsem.at[m, side],
                device_id={"node": place},
                device_id_type=MESH,
            )
            for side in range(2)
        ]

    def own_halo(side):
        return pltpu.make_async_copy(halo_send.at[q, side], halo.at[m, side], own_halo_sem.at[side])

    def borders(d, carry):
        for side, tile in ((0, tile_before(d)), (1, tile_after(d))):
            for k, block in enumerate(pack(rate, tile, side, tile)):
                halo_send[d, side, pl.ds(8 * k, 8), :] = block

        @pl.when(d != q)
        def _():
            for copy in halo_copies(d):
                copy.start()

        @pl.when(d == q)
        def _():
            for side in range(2):
                own_halo(side).start()

        return carry

    lax.fori_loop(0, 4, borders, 0)

    def arrive(j, carry):
        @pl.when(j != m)
        def _():
            def each(slot, inner):
                whole = landed.at[j, slot]
                for part, sem in (
                    (whole.at[:, pl.ds(16, 32)], mid_recv.at[j, slot]),
                    (whole.at[:, pl.ds(0, 16)], end_recv.at[0, j, slot]),
                    (whole.at[:, pl.ds(48, 16)], end_recv.at[1, j, slot]),
                ):
                    pltpu.make_async_remote_copy(
                        src_ref=part,
                        dst_ref=part,
                        send_sem=mid_send.at[0],
                        recv_sem=sem,
                        device_id={"node": (m + 1) % 4},
                        device_id_type=MESH,
                    ).wait_recv()
                return inner

            lax.fori_loop(slot_from, slot_to, each, 0)
            for side in range(2):
                pltpu.make_async_remote_copy(
                    src_ref=halo.at[j, side],
                    dst_ref=halo.at[j, side],
                    send_sem=mid_send.at[0],
                    recv_sem=halo_rsem.at[j, side],
                    device_id={"node": (m + 1) % 4},
                    device_id_type=MESH,
                ).wait_recv()

        @pl.when(j == m)
        def _():
            def each(slot, inner):
                own_copy(slot).wait()
                return inner

            lax.fori_loop(slot_from, slot_to, each, 0)
            for side in range(2):
                own_halo(side).wait()

        return carry

    lax.fori_loop(0, 4, arrive, 0)

    def x_copies2(slot):
        return (
            pltpu.make_async_remote_copy(
                src_ref=u1.at[:, slot + 1, :, pl.ds(48, 16)],
                dst_ref=x_low2.at[slot],
                send_sem=x_send2.at[0, slot],
                recv_sem=x_recv2.at[0, slot],
                device_id={"node": q_up, "space": up},
                device_id_type=MESH,
            ),
            pltpu.make_async_remote_copy(
                src_ref=u1.at[:, slot + 1, :, pl.ds(0, 16)],
                dst_ref=x_high2.at[slot],
                send_sem=x_send2.at[1, slot],
                recv_sem=x_recv2.at[1, slot],
                device_id={"node": q_down, "space": down},
                device_id_type=MESH,
            ),
        )

    def advance(slot, carry):
        def each(part, inner):
            v = part // 8
            at = pl.multiple_of((part % 8) * 8, 8)
            held = [landed[j, slot, v, pl.ds(at, 8), :] for j in range(4)]
            base = start[first_tile + slot, v, pl.ds(at, 8), :]
            for k in range(4):
                total = Q[k][0] * held[0]
                for j in range(1, 4):
                    total = total + Q[k][j] * held[j]
                u1[k, slot + 1, v, pl.ds(at, 8), :] = base + total
            return inner

        lax.fori_loop(0, 40, each, 0)
        one, two = x_copies2(slot)
        one.start()
        two.start()
        return carry

    lax.fori_loop(slot_from, slot_to, advance, 0)

    for side, tile, at in ((0, tile_before(q), slot_from), (1, tile_after(q), slot_to + 1)):
        base = pack(start, tile, side, tile)
        held = [[halo[j, side, pl.ds(8 * k, 8), :] for k in range(10)] for j in range(4)]
        for node in range(4):
            blocks = []
            for k in range(10):
                total = Q[node][0] * held[0][k]
                for j in range(1, 4):
                    total = total + Q[node][j] * held[j][k]
                blocks.append(base[k] + total)
            unpack(blocks, u1.at[node], at, side)

    def inside2(slot, carry):
        def each(node, inner):
            inner_rate(
                u1.at[node],
                slot + 1,
                slot,
                slot + 2,
                rate2.at[node],
                slot,
                first_tile + slot,
            )
            return inner

        lax.fori_loop(0, 4, each, 0)
        return carry

    lax.fori_loop(slot_from, slot_to, inside2, 0)

    def give_copy(node, slot):
        return pltpu.make_async_remote_copy(
            src_ref=give.at[node, slot],
            dst_ref=out_hbm.at[:, :, first_tile + slot, 0, :],
            send_sem=give_send.at[node, slot],
            recv_sem=give_recv.at[first_tile + slot],
            device_id={"node": node},
            device_id_type=MESH,
        )

    def give_here(slot):
        return pltpu.make_async_copy(
            give.at[m, slot], out_hbm.at[:, :, first_tile + slot, 0, :], give_own.at[slot]
        )

    def edges2(slot, carry):
        one, two = x_copies2(slot)
        one.wait_recv()
        two.wait_recv()

        def each(node, inner):
            faces_x(
                u1.at[node],
                slot + 1,
                lambda v, h: x_low2[slot, node, v, pl.ds(8 * h, 8), :],
                slot,
                lambda v, h: x_high2[slot, node, v, pl.ds(8 * h, 8), :],
                slot,
                rate2.at[node],
                slot,
            )
            return inner

        lax.fori_loop(0, 4, each, 0)

        def gather(part, inner):
            v = part // 8
            at = pl.multiple_of((part % 8) * 8, 8)
            held = [rate2[j, slot, v, pl.ds(at, 8), :] for j in range(4)]
            for k in range(4):
                total = Q[k][0] * held[0]
                for j in range(1, 4):
                    total = total + Q[k][j] * held[j]
                give[k, slot, v, pl.ds(at, 8), :] = total
            return inner

        lax.fori_loop(0, 40, gather, 0)

        def send(node, inner):
            @pl.when(node != m)
            def _():
                give_copy(node, slot).start()

            @pl.when(node == m)
            def _():
                give_here(slot).start()

            return inner

        lax.fori_loop(0, 4, send, 0)
        return carry

    lax.fori_loop(slot_from, slot_to, edges2, 0)

    def drain(t, carry):
        one, two = x_copies(t)
        one.wait_send()
        two.wait_send()
        d, place = owner(t)

        @pl.when(d != q)
        def _():
            mid_copy(t).wait_send()
            for copy in end_copies(t):
                copy.wait_send()
            here = out_hbm.at[:, :, t, 0, :]
            pltpu.make_async_remote_copy(
                src_ref=here,
                dst_ref=here,
                send_sem=mid_send.at[0],
                recv_sem=give_recv.at[t],
                device_id={"node": (m + 1) % 4},
                device_id_type=MESH,
            ).wait_recv()

        return carry

    lax.fori_loop(0, TILES, drain, 0)

    def drain_nodes(d, carry):
        @pl.when(d != q)
        def _():
            for copy in halo_copies(d):
                copy.wait_send()

        return carry

    lax.fori_loop(0, 4, drain_nodes, 0)

    def drain_slots(slot, carry):
        one, two = x_copies2(slot)
        one.wait_send()
        two.wait_send()
        give_here(slot).wait()

        def each(node, inner):
            @pl.when(node != m)
            def _():
                give_copy(node, slot).wait_send()

            return inner

        lax.fori_loop(0, 4, each, 0)
        return carry

    lax.fori_loop(slot_from, slot_to, drain_slots, 0)


def body(start_state, node_offset):
    flat = (5, 64, TILES, 1, 128)
    vmem = lambda *shape: pltpu.VMEM(shape, jnp.float32)
    dma = lambda *shape: pltpu.SemaphoreType.DMA(shape)
    out = pl.pallas_call(
        kernel,
        out_shape=jax.ShapeDtypeStruct(flat, jnp.float32),
        in_specs=[pl.BlockSpec(memory_space=pltpu.HBM)] * 2,
        out_specs=pl.BlockSpec(memory_space=pltpu.HBM),
        scratch_shapes=[
            vmem(10, 5, 64, 128),
            vmem(10, 5, 64, 128),
            vmem(10, 5, 16, 128),
            vmem(10, 5, 16, 128),
            vmem(10, 5, 64, 128),
            vmem(4, 2, 80, 128),
            vmem(4, 3, 5, 64, 128),
            vmem(4, 2, 80, 128),
            vmem(4, 5, 5, 64, 128),
            vmem(3, 4, 5, 16, 128),
            vmem(3, 4, 5, 16, 128),
            vmem(4, 3, 5, 64, 128),
            vmem(4, 3, 5, 64, 128),
            dma(2, 10),
            dma(2, 10),
            dma(2, 10),
            dma(10),
            dma(4, 3),
            dma(2, 10),
            dma(2, 4, 3),
            dma(4, 2),
            dma(4, 2),
            dma(3),
            dma(2),
            dma(2, 3),
            dma(2, 3),
            dma(4, 3),
            dma(10),
            dma(3),
        ],
        compiler_params=pltpu.CompilerParams(
            collective_id=0, has_side_effects=True, vmem_limit_bytes=56 << 20
        ),
    )(start_state.reshape(flat), node_offset.reshape(flat))
    return out.reshape((1,) + start_state.shape)


def solution(mesh):
    return jax.shard_map(
        body,
        mesh=mesh,
        in_specs=(
            P(None, None, None, None, "space", None),
            P("node", None, None, None, None, "space", None),
        ),
        out_specs=P("node", None, None, None, None, "space", None),
        check_vma=False,
    )
```

time: 424 us -> 109 us (0.26)
  the two profiles are of different devices: /device:TPU:32 before, /device:TPU:63 now
where the time goes in v1:
time: 109 us
  Pallas kernels  105 us (96%)
  local copies, waits for them, and re-layouts  4.03 us (4%)
    pallas_call x1, Pallas kernels, body(): pl.pallas_call(kernel, out_shape=jax.ShapeDtypeStruct(flat, jnp.float32),...  105 us
    unnamed x1, local copies, waits for them, and re-layouts  4.03 us

profile of v1, /device:TPU:63, one launch (start us, length us, event | category | flops | bytes accessed | tf_op | source)
XLA Modules:
  0.0 108.5 jit_solution(10752301170011157815)
XLA Ops:
  0.0 104.5 %shard_map.28 = f32[5,64,10,1,128]{4,3,2,1,0:T(1,128)} custom-call(f32[5,64,10,1,128]{4,3,2,1,0:T(1,128)} %bitcast.4, f32[5,64,10,1,128]{4,3,2,1,0:T(1,128)} %bitcast.5), custom_call_target="tpu_custom_call" | custom-call | tf_op jit(solution)/shard_map/pallas_call | solution.py:735
  104.5 4.0 %copy.5 = f32[1,5,4,4,4,1,1280]{6,5,4,3,2,1,0:T(1,128)} copy(f32[1,5,4,4,4,1,1280]{6,5,4,3,2,1,0:T(1,128)} %bitcast.3) | data formatting | bytes 3276800

commit v2 on v1

--- a/solution.py
+++ b/solution.py
@@ -239,44 +239,43 @@
     packed = []
     for v in range(5):
         for pair in range(2):
-            c0 = strided(ref, at, v, pair, 0)
-            c3 = strided(ref, at, v, pair, 3)
             if side == 0:
                 one = rows(ref, at, v, 32 * pair + 8)
                 two = rows(ref, at, v, 32 * pair + 24)
                 main = jnp.where(half, swap(one), two)
-                main = jnp.where(lane == 0, turn(c0, 8 + 8 * tile), main)
-                main = jnp.where(lane == 1, turn(c3, 2), main)
             else:
                 one = rows(ref, at, v, 32 * pair)
                 two = rows(ref, at, v, 32 * pair + 16)
                 main = jnp.where(half, one, swap(two))
-                main = jnp.where(lane == 127, turn(c0, 127), main)
-                main = jnp.where(lane == 126, turn(c3, 47 + 8 * tile), main)
+            if tile is not None:
+                c0 = strided(ref, at, v, pair, 0)
+                c3 = strided(ref, at, v, pair, 3)
+                if side == 0:
+                    main = jnp.where(lane == 0, turn(c0, 8 + 8 * tile), main)
+                    main = jnp.where(lane == 1, turn(c3, 2), main)
+                else:
+                    main = jnp.where(lane == 127, turn(c0, 127), main)
+                    main = jnp.where(lane == 126, turn(c3, 47 + 8 * tile), main)
             packed.append(main)
     return packed
 
 
-def unpack(packed, ref, at, side):
+def unpack(packed, ref, at, side, columns):
     for v in range(5):
         for pair in range(2):
             block = packed[2 * v + pair]
-            at0, at3 = (0, 1) if side == 0 else (127, 126)
-            c0 = jnp.broadcast_to(block[:, at0 : at0 + 1], (8, 128))
-            c3 = jnp.broadcast_to(block[:, at3 : at3 + 1], (8, 128))
-            ref[at, v, pl.ds(32 * pair, 8, 4), :] = c0
-            ref[at, v, pl.ds(32 * pair + 3, 8, 4), :] = c3
+            if columns:
+                at0, at3 = (0, 1) if side == 0 else (127, 126)
+                c0 = jnp.broadcast_to(block[:, at0 : at0 + 1], (8, 128))
+                c3 = jnp.broadcast_to(block[:, at3 : at3 + 1], (8, 128))
+                ref[at, v, pl.ds(32 * pair, 8, 4), :] = c0
+                ref[at, v, pl.ds(32 * pair + 3, 8, 4), :] = c3
             shift = 12 if side == 0 else 0
             ref[at, v, pl.ds(32 * pair + shift, 4), :] = block[0:4]
             ref[at, v, pl.ds(32 * pair + 16 + shift, 4), :] = block[4:8]
 
 
-def tile_before(q):
-    return 3 * q - 2 + 11 * ((3 - q) // 3)
-
-
-def tile_after(q):
-    return 3 * q + 2 - 11 * (q // 3)
+MID_FIRST = 1
 
 
 def kernel(
@@ -296,6 +295,8 @@
     x_high2,
     rate2,
     give,
+    pair_send,
+    pair_land,
     load_sem,
     x_send,
     x_recv,
@@ -312,11 +313,15 @@
     give_send,
     give_recv,
     give_own,
+    pair_ssem,
+    pair_rsem,
 ):
     m = lax.axis_index("node")
     s = lax.axis_index("space")
     hi = (s // 8) % 2
     q = m + hi * (3 - 2 * m)
+    odd = q % 2
+    left = 1 - q // 2
     up = (s + 1) % 64
     down = (s + 63) % 64
     hi_up = (up // 8) % 2
@@ -326,6 +331,18 @@
     slot_from = (3 - q) // 3
     slot_to = 3 - q // 3
     first_tile = 3 * q - 1
+    k_from = 1 - (q % 3 + 1) // 2
+    other_q = q + 1 - 2 * odd
+    partner = other_q + hi * (3 - 2 * other_q)
+
+    def turn_of(i):
+        g = i % 5
+        near = (g % 2) * ((g - 1) // 2) + (1 - g % 2) * (4 - g // 2)
+        flip = (i // 5 + left) % 2
+        return near + flip * (9 - 2 * near)
+
+    def place_of(d):
+        return d + hi * (3 - 2 * d)
 
     def loads(t):
         return (
@@ -333,8 +350,8 @@
             pltpu.make_async_copy(offset_hbm.at[:, :, t, 0, :], u0.at[t], load_sem.at[1, t]),
         )
 
-    def begin(t, carry):
-        one, two = loads(t)
+    def begin(i, carry):
+        one, two = loads(turn_of(i))
         one.start()
         two.start()
         return carry
@@ -370,7 +387,8 @@
             ),
         )
 
-    def guess(t, carry):
+    def guess(i, carry):
+        t = turn_of(i)
         one, two = loads(t)
         one.wait()
         two.wait()
@@ -384,29 +402,30 @@
     lax.fori_loop(0, TILES, guess, 0)
 
     def owner(t):
-        d = (t + 1) // 3
-        return d, d + hi * (3 - 2 * d)
+        return (t + 1) // 3
 
     def mid_copy(t):
-        d, place = owner(t)
+        d = owner(t)
+        slot = t - 3 * d + 1
         return pltpu.make_async_remote_copy(
             src_ref=rate.at[t, :, pl.ds(16, 32)],
-            dst_ref=landed.at[m, t - 3 * d + 1, :, pl.ds(16, 32)],
+            dst_ref=landed.at[m, slot, :, pl.ds(16, 32)],
             send_sem=mid_send.at[t],
-            recv_sem=mid_recv.at[m, t - 3 * d + 1],
-            device_id={"node": place},
+            recv_sem=mid_recv.at[m, slot],
+            device_id={"node": place_of(d)},
             device_id_type=MESH,
         )
 
     def end_copies(t):
-        d, place = owner(t)
+        d = owner(t)
+        slot = t - 3 * d + 1
         return [
             pltpu.make_async_remote_copy(
                 src_ref=rate.at[t, :, pl.ds(48 * k, 16)],
-                dst_ref=landed.at[m, t - 3 * d + 1, :, pl.ds(48 * k, 16)],
+                dst_ref=landed.at[m, slot, :, pl.ds(48 * k, 16)],
                 send_sem=end_send.at[k, t],
-                recv_sem=end_recv.at[k, m, t - 3 * d + 1],
-                device_id={"node": place},
+                recv_sem=end_recv.at[k, m, slot],
+                device_id={"node": place_of(d)},
                 device_id_type=MESH,
             )
             for k in range(2)
@@ -417,19 +436,27 @@
             rate.at[first_tile + slot], landed.at[m, slot], own_sem.at[slot]
         )
 
-    def inside(t, carry):
+    def send_mid(i):
+        t = turn_of(i)
+
+        @pl.when(owner(t) != q)
+        def _():
+            mid_copy(t).start()
+
+    def inside(i, carry):
+        t = turn_of(i)
         inner_rate(u0, t, (t + 9) % 10, (t + 1) % 10, rate, t, t)
-        d, place = owner(t)
-
-        @pl.when(d != q)
-        def _():
-            mid_copy(t).start()
+
+        @pl.when(i < MID_FIRST)
+        def _():
+            send_mid(i)
 
         return carry
 
     lax.fori_loop(0, TILES, inside, 0)
 
-    def edges(t, carry):
+    def edges(i, carry):
+        t = turn_of(i)
         one, two = x_copies(t)
         one.wait_recv()
         two.wait_recv()
@@ -443,14 +470,13 @@
             rate,
             t,
         )
-        d, place = owner(t)
-
-        @pl.when(d != q)
+
+        @pl.when(owner(t) != q)
         def _():
             for copy in end_copies(t):
                 copy.start()
 
-        @pl.when(d == q)
+        @pl.when(owner(t) == q)
         def _():
             own_copy(t - first_tile).start()
 
@@ -458,86 +484,47 @@
 
     lax.fori_loop(0, TILES, edges, 0)
 
-    def halo_copies(d):
-        place = d + hi * (3 - 2 * d)
-        return [
-            pltpu.make_async_remote_copy(
-                src_ref=halo_send.at[d, side],
-                dst_ref=halo.at[m, side],
-                send_sem=halo_ssem.at[d, side],
-                recv_sem=halo_rsem.at[m, side],
-                device_id={"node": place},
-                device_id_type=MESH,
-            )
-            for side in range(2)
-        ]
-
-    def own_halo(side):
-        return pltpu.make_async_copy(halo_send.at[q, side], halo.at[m, side], own_halo_sem.at[side])
+    def halo_copy(d):
+        return pltpu.make_async_remote_copy(
+            src_ref=halo_send.at[d],
+            dst_ref=halo.at[m],
+            send_sem=halo_ssem.at[d],
+            recv_sem=halo_rsem.at[m],
+            device_id={"node": place_of(d)},
+            device_id_type=MESH,
+        )
+
+    own_halo = pltpu.make_async_copy(halo_send.at[q], halo.at[m], own_halo_sem)
+
+    for d, side, tile in ((0, 0, 9), (1, 1, 5), (2, 0, 4), (3, 1, 0)):
+        for k, block in enumerate(pack(rate, tile, side, None)):
+            halo_send[d, pl.ds(8 * k, 8), :] = block
 
     def borders(d, carry):
-        for side, tile in ((0, tile_before(d)), (1, tile_after(d))):
-            for k, block in enumerate(pack(rate, tile, side, tile)):
-                halo_send[d, side, pl.ds(8 * k, 8), :] = block
-
         @pl.when(d != q)
         def _():
-            for copy in halo_copies(d):
-                copy.start()
-
-        @pl.when(d == q)
-        def _():
-            for side in range(2):
-                own_halo(side).start()
+            halo_copy(d).start()
 
         return carry
 
     lax.fori_loop(0, 4, borders, 0)
-
-    def arrive(j, carry):
-        @pl.when(j != m)
-        def _():
-            def each(slot, inner):
-                whole = landed.at[j, slot]
-                for part, sem in (
-                    (whole.at[:, pl.ds(16, 32)], mid_recv.at[j, slot]),
-                    (whole.at[:, pl.ds(0, 16)], end_recv.at[0, j, slot]),
-                    (whole.at[:, pl.ds(48, 16)], end_recv.at[1, j, slot]),
-                ):
-                    pltpu.make_async_remote_copy(
-                        src_ref=part,
-                        dst_ref=part,
-                        send_sem=mid_send.at[0],
-                        recv_sem=sem,
-                        device_id={"node": (m + 1) % 4},
-                        device_id_type=MESH,
-                    ).wait_recv()
-                return inner
-
-            lax.fori_loop(slot_from, slot_to, each, 0)
-            for side in range(2):
-                pltpu.make_async_remote_copy(
-                    src_ref=halo.at[j, side],
-                    dst_ref=halo.at[j, side],
-                    send_sem=mid_send.at[0],
-                    recv_sem=halo_rsem.at[j, side],
-                    device_id={"node": (m + 1) % 4},
-                    device_id_type=MESH,
-                ).wait_recv()
-
-        @pl.when(j == m)
-        def _():
-            def each(slot, inner):
-                own_copy(slot).wait()
-                return inner
-
-            lax.fori_loop(slot_from, slot_to, each, 0)
-            for side in range(2):
-                own_halo(side).wait()
-
-        return carry
-
-    lax.fori_loop(0, 4, arrive, 0)
+    own_halo.start()
+
+    def rest(i, carry):
+        send_mid(i)
+        return carry
+
+    lax.fori_loop(MID_FIRST, TILES, rest, 0)
+
+    def arrived(part, sem):
+        pltpu.make_async_remote_copy(
+            src_ref=part,
+            dst_ref=part,
+            send_sem=mid_send.at[0],
+            recv_sem=sem,
+            device_id={"node": (m + 1) % 4},
+            device_id_type=MESH,
+        ).wait_recv()
 
     def x_copies2(slot):
         return (
@@ -559,56 +546,125 @@
             ),
         )
 
-    def advance(slot, carry):
-        def each(part, inner):
-            v = part // 8
-            at = pl.multiple_of((part % 8) * 8, 8)
-            held = [landed[j, slot, v, pl.ds(at, 8), :] for j in range(4)]
-            base = start[first_tile + slot, v, pl.ds(at, 8), :]
-            for k in range(4):
-                total = Q[k][0] * held[0]
-                for j in range(1, 4):
-                    total = total + Q[k][j] * held[j]
-                u1[k, slot + 1, v, pl.ds(at, 8), :] = base + total
+    def advance(slot, offset, stride):
+        def each(v, inner):
+            for part in range(4):
+                at = offset + 8 * (part % 2) + stride * (part // 2)
+                held = [landed[j, slot, v, pl.ds(at, 8), :] for j in range(4)]
+                base = start[first_tile + slot, v, pl.ds(at, 8), :]
+                for k in range(4):
+                    total = Q[k][0] * held[0]
+                    for j in range(1, 4):
+                        total = total + Q[k][j] * held[j]
+                    u1[k, slot + 1, v, pl.ds(at, 8), :] = base + total
             return inner
 
-        lax.fori_loop(0, 40, each, 0)
+        lax.fori_loop(0, 5, each, 0)
+
+    def next_state(slot):
+        def ends(j, carry):
+            @pl.when(j != m)
+            def _():
+                for k in range(2):
+                    arrived(landed.at[j, slot, :, pl.ds(48 * k, 16)], end_recv.at[k, j, slot])
+
+            return carry
+
+        own_copy(slot).wait()
+        lax.fori_loop(0, 4, ends, 0)
+        advance(slot, 0, 48)
         one, two = x_copies2(slot)
         one.start()
         two.start()
-        return carry
-
-    lax.fori_loop(slot_from, slot_to, advance, 0)
-
-    for side, tile, at in ((0, tile_before(q), slot_from), (1, tile_after(q), slot_to + 1)):
-        base = pack(start, tile, side, tile)
-        held = [[halo[j, side, pl.ds(8 * k, 8), :] for k in range(10)] for j in range(4)]
-        for node in range(4):
-            blocks = []
-            for k in range(10):
-                total = Q[node][0] * held[0][k]
-                for j in range(1, 4):
-                    total = total + Q[node][j] * held[j][k]
-                blocks.append(base[k] + total)
-            unpack(blocks, u1.at[node], at, side)
-
-    def inside2(slot, carry):
-        def each(node, inner):
-            inner_rate(
-                u1.at[node],
-                slot + 1,
-                slot,
-                slot + 2,
-                rate2.at[node],
-                slot,
-                first_tile + slot,
-            )
-            return inner
-
-        lax.fori_loop(0, 4, each, 0)
-        return carry
-
-    lax.fori_loop(slot_from, slot_to, inside2, 0)
+
+        def mids(j, carry):
+            @pl.when(j != m)
+            def _():
+                arrived(landed.at[j, slot, :, pl.ds(16, 32)], mid_recv.at[j, slot])
+
+            return carry
+
+        lax.fori_loop(0, 4, mids, 0)
+        advance(slot, 16, 16)
+
+    def middle_rows():
+        def wait(j, carry):
+            @pl.when(j != m)
+            def _():
+                arrived(halo.at[j], halo_rsem.at[j])
+
+            return carry
+
+        own_halo.wait()
+        lax.fori_loop(0, 4, wait, 0)
+
+        def fill(side, tile, at):
+            base = pack(start, tile, side, None)
+            held = [[halo[j, pl.ds(8 * k, 8), :] for k in range(10)] for j in range(4)]
+            for node in range(4):
+                blocks = []
+                for k in range(10):
+                    total = Q[node][0] * held[0][k]
+                    for j in range(1, 4):
+                        total = total + Q[node][j] * held[j][k]
+                    blocks.append(base[k] + total)
+                unpack(blocks, u1.at[node], at, side, False)
+
+        @pl.when(odd == 0)
+        def _():
+            fill(0, (first_tile + slot_from + 9) % 10, slot_from)
+
+        @pl.when(odd == 1)
+        def _():
+            fill(1, (first_tile + slot_to) % 10, slot_to + 1)
+
+    pair_copy = pltpu.make_async_remote_copy(
+        src_ref=pair_send,
+        dst_ref=pair_land,
+        send_sem=pair_ssem,
+        recv_sem=pair_rsem,
+        device_id={"node": partner},
+        device_id_type=MESH,
+    )
+
+    def pair_out(slot):
+        def give_rows(side):
+            def each(node, carry):
+                blocks = pack(u1.at[node], slot + 1, side, first_tile + slot)
+                for k, block in enumerate(blocks):
+                    pair_send[node, pl.ds(8 * k, 8), :] = block
+                return carry
+
+            lax.fori_loop(0, 4, each, 0)
+
+        @pl.when(odd == 0)
+        def _():
+            give_rows(0)
+
+        @pl.when(odd == 1)
+        def _():
+            give_rows(1)
+
+        pair_copy.start()
+
+    def pair_in():
+        pair_copy.wait_recv()
+
+        def take_rows(side, at):
+            def each(node, carry):
+                blocks = [pair_land[node, pl.ds(8 * k, 8), :] for k in range(10)]
+                unpack(blocks, u1.at[node], at, side, True)
+                return carry
+
+            lax.fori_loop(0, 4, each, 0)
+
+        @pl.when(odd == 0)
+        def _():
+            take_rows(1, slot_to + 1)
+
+        @pl.when(odd == 1)
+        def _():
+            take_rows(0, slot_from)
 
     def give_copy(node, slot):
         return pltpu.make_async_remote_copy(
@@ -625,12 +681,19 @@
             give.at[m, slot], out_hbm.at[:, :, first_tile + slot, 0, :], give_own.at[slot]
         )
 
-    def edges2(slot, carry):
+    def second(slot):
+        def each(node, carry):
+            inner_rate(
+                u1.at[node], slot + 1, slot, slot + 2, rate2.at[node], slot, first_tile + slot
+            )
+            return carry
+
+        lax.fori_loop(0, 4, each, 0)
         one, two = x_copies2(slot)
         one.wait_recv()
         two.wait_recv()
 
-        def each(node, inner):
+        def edge(node, carry):
             faces_x(
                 u1.at[node],
                 slot + 1,
@@ -641,24 +704,25 @@
                 rate2.at[node],
                 slot,
             )
-            return inner
-
-        lax.fori_loop(0, 4, each, 0)
-
-        def gather(part, inner):
-            v = part // 8
-            at = pl.multiple_of((part % 8) * 8, 8)
-            held = [rate2[j, slot, v, pl.ds(at, 8), :] for j in range(4)]
-            for k in range(4):
-                total = Q[k][0] * held[0]
-                for j in range(1, 4):
-                    total = total + Q[k][j] * held[j]
-                give[k, slot, v, pl.ds(at, 8), :] = total
-            return inner
-
-        lax.fori_loop(0, 40, gather, 0)
-
-        def send(node, inner):
+            return carry
+
+        lax.fori_loop(0, 4, edge, 0)
+
+        def gather(v, carry):
+            for part in range(8):
+                held = [rate2[j, slot, v, pl.ds(8 * part, 8), :] for j in range(4)]
+                for k in range(4):
+                    total = Q[k][0] * held[0]
+                    for j in range(1, 4):
+                        total = total + Q[k][j] * held[j]
+                    give[k, slot, v, pl.ds(8 * part, 8), :] = total
+            return carry
+
+        lax.fori_loop(0, 5, gather, 0)
+
+        def send(k, carry):
+            node = (m + 2 + k) % 4
+
             @pl.when(node != m)
             def _():
                 give_copy(node, slot).start()
@@ -667,33 +731,49 @@
             def _():
                 give_here(slot).start()
 
-            return inner
+            return carry
 
         lax.fori_loop(0, 4, send, 0)
-        return carry
-
-    lax.fori_loop(slot_from, slot_to, edges2, 0)
+
+    def slot_of(k):
+        return k + odd * (2 - 2 * k)
+
+    def stage(k, carry):
+        @pl.when(k < 3)
+        def _():
+            next_state(slot_of(k))
+
+        @pl.when(k == k_from)
+        def _():
+            middle_rows()
+
+        @pl.when(k == 2)
+        def _():
+            pair_out(slot_of(k))
+
+        @pl.when(k == 3)
+        def _():
+            pair_in()
+
+        @pl.when(k > k_from)
+        def _():
+            second(slot_of(k - 1))
+
+        return carry
+
+    lax.fori_loop(k_from, 4, stage, 0)
 
     def drain(t, carry):
         one, two = x_copies(t)
         one.wait_send()
         two.wait_send()
-        d, place = owner(t)
-
-        @pl.when(d != q)
+
+        @pl.when(owner(t) != q)
         def _():
             mid_copy(t).wait_send()
             for copy in end_copies(t):
                 copy.wait_send()
-            here = out_hbm.at[:, :, t, 0, :]
-            pltpu.make_async_remote_copy(
-                src_ref=here,
-                dst_ref=here,
-                send_sem=mid_send.at[0],
-                recv_sem=give_recv.at[t],
-                device_id={"node": (m + 1) % 4},
-                device_id_type=MESH,
-            ).wait_recv()
+            arrived(out_hbm.at[:, :, t, 0, :], give_recv.at[t])
 
         return carry
 
@@ -702,12 +782,12 @@
     def drain_nodes(d, carry):
         @pl.when(d != q)
         def _():
-            for copy in halo_copies(d):
-                copy.wait_send()
+            halo_copy(d).wait_send()
 
         return carry
 
     lax.fori_loop(0, 4, drain_nodes, 0)
+    pair_copy.wait_send()
 
     def drain_slots(slot, carry):
         one, two = x_copies2(slot)
@@ -736,21 +816,23 @@
         kernel,
         out_shape=jax.ShapeDtypeStruct(flat, jnp.float32),
         in_specs=[pl.BlockSpec(memory_space=pltpu.HBM)] * 2,
-        out_specs=pl.BlockSpec(memory_space=pltpu.HBM),
+        out_specs=pl.BlockSpec(memory_space=pl.ANY),
         scratch_shapes=[
             vmem(10, 5, 64, 128),
             vmem(10, 5, 64, 128),
             vmem(10, 5, 16, 128),
             vmem(10, 5, 16, 128),
             vmem(10, 5, 64, 128),
-            vmem(4, 2, 80, 128),
+            vmem(4, 80, 128),
             vmem(4, 3, 5, 64, 128),
-            vmem(4, 2, 80, 128),
+            vmem(4, 80, 128),
             vmem(4, 5, 5, 64, 128),
             vmem(3, 4, 5, 16, 128),
             vmem(3, 4, 5, 16, 128),
             vmem(4, 3, 5, 64, 128),
             vmem(4, 3, 5, 64, 128),
+            vmem(4, 80, 128),
+            vmem(4, 80, 128),
             dma(2, 10),
             dma(2, 10),
             dma(2, 10),
@@ -758,18 +840,20 @@
             dma(4, 3),
             dma(2, 10),
             dma(2, 4, 3),
-            dma(4, 2),
-            dma(4, 2),
+            dma(4),
+            dma(4),
             dma(3),
-            dma(2),
+            pltpu.SemaphoreType.DMA,
             dma(2, 3),
             dma(2, 3),
             dma(4, 3),
             dma(10),
             dma(3),
+            pltpu.SemaphoreType.DMA,
+            pltpu.SemaphoreType.DMA,
         ],
         compiler_params=pltpu.CompilerParams(
-            collective_id=0, has_side_effects=True, vmem_limit_bytes=56 << 20
+            collective_id=0, has_side_effects=True, vmem_limit_bytes=52 << 20
         ),
     )(start_state.reshape(flat), node_offset.reshape(flat))
     return out.reshape((1,) + start_state.shape)

time: 109 us -> 95.2 us (0.87)
  the two profiles are of different devices: /device:TPU:63 before, /device:TPU:32 now
where the time goes in v2:
time: 95.2 us; the launch traced here: 95.1 us
  Pallas kernels  93.9 us (99%)
  local copies, waits for them, and re-layouts  1.17 us (1%)
    pallas_call x1, Pallas kernels, body(): pl.pallas_call(kernel, out_shape=jax.ShapeDtypeStruct(flat, jnp.float32),...  93.9 us

profile of v2, /device:TPU:32, one launch (start us, length us, event | category | flops | bytes accessed | tf_op | source)
XLA Modules:
  0.0 95.1 jit_solution(4582738914773801993)
XLA Ops:
  0.0 93.9 %shard_map.28 = f32[5,64,10,1,128]{4,3,2,1,0:T(1,128)S(1)} custom-call(f32[5,64,10,1,128]{4,3,2,1,0:T(1,128)} %bitcast.4, f32[5,64,10,1,128]{4,3,2,1,0:T(1,128)} %bitcast.5), custom_call_target="tpu_custom_call" | custom-call | tf_op jit(solution)/shard_map/pallas_call | solution.py:815
  93.9 1.2 %copy.5 = f32[1,5,4,4,4,1,1280]{6,5,4,3,2,1,0:T(1,128)} copy(f32[1,5,4,4,4,1,1280]{6,5,4,3,2,1,0:T(1,128)S(1)} %bitcast.3) | data formatting | bytes 3276800

commit v3 on v2

--- a/solution.py
+++ b/solution.py
@@ -275,7 +275,13 @@
             ref[at, v, pl.ds(32 * pair + 16 + shift, 4), :] = block[4:8]
 
 
-MID_FIRST = 1
+MID_FIRST = 3
+HELPER = -2
+ONWARD = 1 - HELPER
+
+
+def relayed(t):
+    return (t == 1) | (t == 2) | (t == 3) | (t == 7) | (t == 8) | (t == 6)
 
 
 def kernel(
@@ -297,6 +303,7 @@
     give,
     pair_send,
     pair_land,
+    relay,
     load_sem,
     x_send,
     x_recv,
@@ -315,6 +322,9 @@
     give_own,
     pair_ssem,
     pair_rsem,
+    relay_send,
+    relay_recv,
+    onward_send,
 ):
     m = lax.axis_index("node")
     s = lax.axis_index("space")
@@ -334,6 +344,13 @@
     k_from = 1 - (q % 3 + 1) // 2
     other_q = q + 1 - 2 * odd
     partner = other_q + hi * (3 - 2 * other_q)
+    far_up = s % 8 == 7
+    far_down = s % 8 == 0
+    helps_up = s % 8 == (7 + HELPER) % 8
+    helps_down = s % 8 == (-HELPER) % 8
+
+    def space(distance):
+        return (s + 64 + distance) % 64
 
     def turn_of(i):
         g = i % 5
@@ -365,7 +382,30 @@
     pl.semaphore_signal(barrier, inc=1, device_id={"space": down}, device_id_type=MESH)
     pl.semaphore_signal(barrier, inc=1, device_id={"node": q_up, "space": up}, device_id_type=MESH)
     pl.semaphore_signal(barrier, inc=1, device_id={"node": q_down, "space": down}, device_id_type=MESH)
-    pl.semaphore_wait(barrier, 7)
+    for role, friends in (
+        (far_up, (HELPER, 1 - HELPER)),
+        (far_down, (-HELPER, HELPER - 1)),
+        (helps_up, (-HELPER, ONWARD)),
+        (helps_down, (HELPER, -ONWARD)),
+    ):
+
+        @pl.when(role)
+        def _(friends=friends):
+            for friend in friends:
+                pl.semaphore_signal(
+                    barrier, inc=1, device_id={"space": space(friend)}, device_id_type=MESH
+                )
+
+    in_relay = far_up | far_down | helps_up | helps_down
+
+    @pl.when(in_relay)
+    def _():
+        pl.semaphore_wait(barrier, 9)
+
+    @pl.when(jnp.logical_not(in_relay))
+    def _():
+        pl.semaphore_wait(barrier, 7)
+
 
     def x_copies(t):
         return (
@@ -387,6 +427,46 @@
             ),
         )
 
+    def relay_copies(t):
+        return (
+            pltpu.make_async_remote_copy(
+                src_ref=u0.at[t, :, pl.ds(48, 16)],
+                dst_ref=relay.at[t],
+                send_sem=relay_send.at[t],
+                recv_sem=relay_recv.at[t],
+                device_id={"space": space(HELPER)},
+                device_id_type=MESH,
+            ),
+            pltpu.make_async_remote_copy(
+                src_ref=u0.at[t, :, pl.ds(0, 16)],
+                dst_ref=relay.at[t],
+                send_sem=relay_send.at[t],
+                recv_sem=relay_recv.at[t],
+                device_id={"space": space(-HELPER)},
+                device_id_type=MESH,
+            ),
+        )
+
+    def onward_copies(t):
+        return (
+            pltpu.make_async_remote_copy(
+                src_ref=relay.at[t],
+                dst_ref=x_low.at[t],
+                send_sem=onward_send.at[t],
+                recv_sem=x_recv.at[0, t],
+                device_id={"space": space(ONWARD)},
+                device_id_type=MESH,
+            ),
+            pltpu.make_async_remote_copy(
+                src_ref=relay.at[t],
+                dst_ref=x_high.at[t],
+                send_sem=onward_send.at[t],
+                recv_sem=x_recv.at[1, t],
+                device_id={"space": space(-ONWARD)},
+                device_id_type=MESH,
+            ),
+        )
+
     def guess(i, carry):
         t = turn_of(i)
         one, two = loads(t)
@@ -395,8 +475,24 @@
         for v in range(5):
             u0[t, v] = u0[t, v] + start[t, v]
         one, two = x_copies(t)
-        one.start()
-        two.start()
+        by_up, by_down = relay_copies(t)
+
+        @pl.when(far_up & relayed(t))
+        def _():
+            by_up.start()
+
+        @pl.when(jnp.logical_not(far_up & relayed(t)))
+        def _():
+            one.start()
+
+        @pl.when(far_down & relayed(t))
+        def _():
+            by_down.start()
+
+        @pl.when(jnp.logical_not(far_down & relayed(t)))
+        def _():
+            two.start()
+
         return carry
 
     lax.fori_loop(0, TILES, guess, 0)
@@ -454,6 +550,23 @@
         return carry
 
     lax.fori_loop(0, TILES, inside, 0)
+
+    def onward(t, carry):
+        one, two = onward_copies(t)
+
+        @pl.when(helps_up & relayed(t))
+        def _():
+            relay_copies(t)[0].wait_recv()
+            one.start()
+
+        @pl.when(helps_down & relayed(t))
+        def _():
+            relay_copies(t)[1].wait_recv()
+            two.start()
+
+        return carry
+
+    lax.fori_loop(1, 9, onward, 0)
 
     def edges(i, carry):
         t = turn_of(i)
@@ -765,8 +878,32 @@
 
     def drain(t, carry):
         one, two = x_copies(t)
-        one.wait_send()
-        two.wait_send()
+        by_up, by_down = relay_copies(t)
+        on_up, on_down = onward_copies(t)
+
+        @pl.when(far_up & relayed(t))
+        def _():
+            by_up.wait_send()
+
+        @pl.when(jnp.logical_not(far_up & relayed(t)))
+        def _():
+            one.wait_send()
+
+        @pl.when(far_down & relayed(t))
+        def _():
+            by_down.wait_send()
+
+        @pl.when(jnp.logical_not(far_down & relayed(t)))
+        def _():
+            two.wait_send()
+
+        @pl.when(helps_up & relayed(t))
+        def _():
+            on_up.wait_send()
+
+        @pl.when(helps_down & relayed(t))
+        def _():
+            on_down.wait_send()
 
         @pl.when(owner(t) != q)
         def _():
@@ -833,6 +970,7 @@
             vmem(4, 3, 5, 64, 128),
             vmem(4, 80, 128),
             vmem(4, 80, 128),
+            vmem(10, 5, 16, 128),
             dma(2, 10),
             dma(2, 10),
             dma(2, 10),
@@ -851,6 +989,9 @@
             dma(3),
             pltpu.SemaphoreType.DMA,
             pltpu.SemaphoreType.DMA,
+            dma(10),
+            dma(10),
+            dma(10),
         ],
         compiler_params=pltpu.CompilerParams(
             collective_id=0, has_side_effects=True, vmem_limit_bytes=52 << 20

time: 95.2 us -> 90.9 us (0.955)
  Pallas kernels: 93.9 us -> 89.6 us
    pallas_call x1, Pallas kernels: 93.9 us -> 89.6 us  [body(): pl.pallas_call(kernel, out_shape=jax.ShapeDtypeStruct(flat, jnp.float32),...]
where the time goes in v3:
time: 90.9 us; the launch traced here: 90.8 us
  Pallas kernels  89.6 us (99%)
  local copies, waits for them, and re-layouts  1.17 us (1%)
    pallas_call x1, Pallas kernels, body(): pl.pallas_call(kernel, out_shape=jax.ShapeDtypeStruct(flat, jnp.float32),...  89.6 us

profile of v3, /device:TPU:32, one launch (start us, length us, event | category | flops | bytes accessed | tf_op | source)
XLA Modules:
  0.0 90.8 jit_solution(11044484669656748378)
XLA Ops:
  0.0 89.6 %shard_map.28 = f32[5,64,10,1,128]{4,3,2,1,0:T(1,128)S(1)} custom-call(f32[5,64,10,1,128]{4,3,2,1,0:T(1,128)} %bitcast.4, f32[5,64,10,1,128]{4,3,2,1,0:T(1,128)} %bitcast.5), custom_call_target="tpu_custom_call" | custom-call | tf_op jit(solution)/shard_map/pallas_call | solution.py:952
  89.6 1.2 %copy.5 = f32[1,5,4,4,4,1,1280]{6,5,4,3,2,1,0:T(1,128)} copy(f32[1,5,4,4,4,1,1280]{6,5,4,3,2,1,0:T(1,128)S(1)} %bitcast.3) | data formatting | bytes 3276800

commit v4 on v3

--- a/solution.py
+++ b/solution.py
@@ -273,6 +273,35 @@
             shift = 12 if side == 0 else 0
             ref[at, v, pl.ds(32 * pair + shift, 4), :] = block[0:4]
             ref[at, v, pl.ds(32 * pair + 16 + shift, 4), :] = block[4:8]
+
+
+def squeeze(packed, side):
+    lane = lanes()
+    blocks = [turn(block, 80) for block in packed] if side == 0 else packed
+    full = [jnp.where(lane < 64, blocks[2 * i], turn(blocks[2 * i + 1], 64)) for i in range(5)]
+    for group in (range(8), range(8, 10)):
+        tail = turn(blocks[group[0]], 64)
+        for g, k in enumerate(group):
+            if g:
+                tail = jnp.where(lane >= 16 * g, turn(blocks[k], (64 + 16 * g) % 128), tail)
+        full.append(tail)
+    return full
+
+
+def stretch(full, side):
+    lane = lanes()
+    packed = []
+    for k in range(10):
+        main = full[k // 2]
+        if k % 2:
+            main = turn(main, 64)
+        tail = full[5 + k // 8]
+        shift = (64 - 16 * (k % 8)) % 128
+        if shift:
+            tail = turn(tail, shift)
+        block = jnp.where(lane < 64, main, tail)
+        packed.append(turn(block, 48) if side == 0 else block)
+    return packed
 
 
 MID_FIRST = 3
@@ -610,7 +639,7 @@
     own_halo = pltpu.make_async_copy(halo_send.at[q], halo.at[m], own_halo_sem)
 
     for d, side, tile in ((0, 0, 9), (1, 1, 5), (2, 0, 4), (3, 1, 0)):
-        for k, block in enumerate(pack(rate, tile, side, None)):
+        for k, block in enumerate(squeeze(pack(rate, tile, side, None), side)):
             halo_send[d, pl.ds(8 * k, 8), :] = block
 
     def borders(d, carry):
@@ -712,16 +741,16 @@
         lax.fori_loop(0, 4, wait, 0)
 
         def fill(side, tile, at):
-            base = pack(start, tile, side, None)
-            held = [[halo[j, pl.ds(8 * k, 8), :] for k in range(10)] for j in range(4)]
+            base = squeeze(pack(start, tile, side, None), side)
+            held = [[halo[j, pl.ds(8 * k, 8), :] for k in range(7)] for j in range(4)]
             for node in range(4):
                 blocks = []
-                for k in range(10):
+                for k in range(7):
                     total = Q[node][0] * held[0][k]
                     for j in range(1, 4):
                         total = total + Q[node][j] * held[j][k]
                     blocks.append(base[k] + total)
-                unpack(blocks, u1.at[node], at, side, False)
+                unpack(stretch(blocks, side), u1.at[node], at, side, False)
 
         @pl.when(odd == 0)
         def _():
@@ -856,13 +885,13 @@
         def _():
             next_state(slot_of(k))
 
-        @pl.when(k == k_from)
+        @pl.when(k == 2)
+        def _():
+            pair_out(slot_of(k))
+
+        @pl.when(k == k_from + 1)
         def _():
             middle_rows()
-
-        @pl.when(k == 2)
-        def _():
-            pair_out(slot_of(k))
 
         @pl.when(k == 3)
         def _():
@@ -960,9 +989,9 @@
             vmem(10, 5, 16, 128),
             vmem(10, 5, 16, 128),
             vmem(10, 5, 64, 128),
-            vmem(4, 80, 128),
+            vmem(4, 56, 128),
             vmem(4, 3, 5, 64, 128),
-            vmem(4, 80, 128),
+            vmem(4, 56, 128),
             vmem(4, 5, 5, 64, 128),
             vmem(3, 4, 5, 16, 128),
             vmem(3, 4, 5, 16, 128),

time: 90.9 us -> 89.3 us (0.982)
  Pallas kernels: 89.6 us -> 87.3 us
    pallas_call x1, Pallas kernels: 89.6 us -> 87.3 us  [body(): pl.pallas_call(kernel, out_shape=jax.ShapeDtypeStruct(flat, jnp.float32),...]
where the time goes in v4:
time: 89.3 us; the launch traced here: 88.5 us
  Pallas kernels  87.3 us (98%)
  local copies, waits for them, and re-layouts  1.17 us (1%)
    pallas_call x1, Pallas kernels, body(): pl.pallas_call(kernel, out_shape=jax.ShapeDtypeStruct(flat, jnp.float32),...  87.3 us

profile of v4, /device:TPU:32, one launch (start us, length us, event | category | flops | bytes accessed | tf_op | source)
XLA Modules:
  0.0 88.5 jit_solution(5882166215054391261)
XLA Ops:
  0.0 87.3 %shard_map.28 = f32[5,64,10,1,128]{4,3,2,1,0:T(1,128)S(1)} custom-call(f32[5,64,10,1,128]{4,3,2,1,0:T(1,128)} %bitcast.4, f32[5,64,10,1,128]{4,3,2,1,0:T(1,128)} %bitcast.5), custom_call_target="tpu_custom_call" | custom-call | tf_op jit(solution)/shard_map/pallas_call | solution.py:981
  87.3 1.2 %copy.5 = f32[1,5,4,4,4,1,1280]{6,5,4,3,2,1,0:T(1,128)} copy(f32[1,5,4,4,4,1,1280]{6,5,4,3,2,1,0:T(1,128)S(1)} %bitcast.3) | data formatting | bytes 3276800

commit v5 on v4

--- a/solution.py
+++ b/solution.py
@@ -568,6 +568,21 @@
         def _():
             mid_copy(t).start()
 
+    def onward(t, carry):
+        one, two = onward_copies(t)
+
+        @pl.when(helps_up & relayed(t))
+        def _():
+            relay_copies(t)[0].wait_recv()
+            one.start()
+
+        @pl.when(helps_down & relayed(t))
+        def _():
+            relay_copies(t)[1].wait_recv()
+            two.start()
+
+        return carry
+
     def inside(i, carry):
         t = turn_of(i)
         inner_rate(u0, t, (t + 9) % 10, (t + 1) % 10, rate, t, t)
@@ -576,26 +591,14 @@
         def _():
             send_mid(i)
 
+        @pl.when(i == 6)
+        def _():
+            lax.fori_loop(1, 9, onward, 0)
+
         return carry
 
     lax.fori_loop(0, TILES, inside, 0)
 
-    def onward(t, carry):
-        one, two = onward_copies(t)
-
-        @pl.when(helps_up & relayed(t))
-        def _():
-            relay_copies(t)[0].wait_recv()
-            one.start()
-
-        @pl.when(helps_down & relayed(t))
-        def _():
-            relay_copies(t)[1].wait_recv()
-            two.start()
-
-        return carry
-
-    lax.fori_loop(1, 9, onward, 0)
 
     def edges(i, carry):
         t = turn_of(i)

time: 89.3 us -> 89.3 us (level)
  no operation moved by 1% of the time
where the time goes in v5:
time: 89.3 us; the launch traced here: 88.5 us
  Pallas kernels  87.3 us (98%)
  local copies, waits for them, and re-layouts  1.17 us (1%)
    pallas_call x1, Pallas kernels, body(): pl.pallas_call(kernel, out_shape=jax.ShapeDtypeStruct(flat, jnp.float32),...  87.3 us

profile of v5, /device:TPU:32, one launch (start us, length us, event | category | flops | bytes accessed | tf_op | source)
XLA Modules:
  0.0 88.5 jit_solution(9727709847688782905)
XLA Ops:
  0.0 87.3 %shard_map.28 = f32[5,64,10,1,128]{4,3,2,1,0:T(1,128)S(1)} custom-call(f32[5,64,10,1,128]{4,3,2,1,0:T(1,128)} %bitcast.4, f32[5,64,10,1,128]{4,3,2,1,0:T(1,128)} %bitcast.5), custom_call_target="tpu_custom_call" | custom-call | tf_op jit(solution)/shard_map/pallas_call | solution.py:984
  87.3 1.2 %copy.5 = f32[1,5,4,4,4,1,1280]{6,5,4,3,2,1,0:T(1,128)} copy(f32[1,5,4,4,4,1,1280]{6,5,4,3,2,1,0:T(1,128)S(1)} %bitcast.3) | data formatting | bytes 3276800

commit v6 on v5

--- a/solution.py
+++ b/solution.py
@@ -866,7 +866,7 @@
         lax.fori_loop(0, 5, gather, 0)
 
         def send(k, carry):
-            node = (m + 2 + k) % 4
+            node = (3 - k) * (1 - m // 2) + k * (m // 2)
 
             @pl.when(node != m)
             def _():

time: 89.3 us -> 89.3 us (level)
  no operation moved by 1% of the time
where the time goes in v6:
time: 89.3 us; the launch traced here: 88.5 us
  Pallas kernels  87.3 us (98%)
  local copies, waits for them, and re-layouts  1.17 us (1%)
    pallas_call x1, Pallas kernels, body(): pl.pallas_call(kernel, out_shape=jax.ShapeDtypeStruct(flat, jnp.float32),...  87.3 us

profile of v6, /device:TPU:32, one launch (start us, length us, event | category | flops | bytes accessed | tf_op | source)
XLA Modules:
  0.0 88.5 jit_solution(401929018182260098)
XLA Ops:
  0.0 87.3 %shard_map.28 = f32[5,64,10,1,128]{4,3,2,1,0:T(1,128)S(1)} custom-call(f32[5,64,10,1,128]{4,3,2,1,0:T(1,128)} %bitcast.4, f32[5,64,10,1,128]{4,3,2,1,0:T(1,128)} %bitcast.5), custom_call_target="tpu_custom_call" | custom-call | tf_op jit(solution)/shard_map/pallas_call | solution.py:984
  87.3 1.2 %copy.5 = f32[1,5,4,4,4,1,1280]{6,5,4,3,2,1,0:T(1,128)} copy(f32[1,5,4,4,4,1,1280]{6,5,4,3,2,1,0:T(1,128)S(1)} %bitcast.3) | data formatting | bytes 3276800
